TPU v7x, 32 devices: a whole 2x2x4 slice. The times are simulated.
32 devices in a mesh: replica: 4 (over y, x), group: 8 (over z, core).
Axes of the slice: x: 2, y: 2, z: 4, core: 2. Of those that a mesh axis runs over, the one named last changes fastest.
Arguments:
- tokens: float32 [16384, 384], P(('replica', 'group')), may hold values from -6 to 6
- image_count: int32 [4], replicated, may hold values from 10 to 20, as said below
- w_qkv: float32 [384, 1152], P(None, 'group'), may hold values from -0.3125 to 0.3125
- w_out: float32 [384, 384], P(None, 'group'), may hold values from -1.75 to 1.75
- w_up: float32 [384, 1536], P(None, 'group'), may hold values from -0.3125 to 0.3125
- w_down: float32 [1536, 384], P('group'), may hold values from -0.15625 to 0.15625
- vectors: float32 [12, 384], P(None, 'group'), may hold values from -2 to 2
- cotangent: float32 [16384, 384], P(('replica', 'group')), may hold values from -6 to 6
- mom_qkv: float32 [384, 1152], P(None, 'group'), may hold values from -384 to 384
- mom_out: float32 [384, 384], P(None, 'group'), may hold values from -384 to 384
- mom_up: float32 [384, 1536], P(None, 'group'), may hold values from -384 to 384
- mom_down: float32 [1536, 384], P('group'), may hold values from -384 to 384
- mom_vectors: float32 [12, 384], P(None, 'group'), may hold values from -384 to 384
Outputs:
- block_out: float32 [16384, 384], P(('replica', 'group'))
- grad_tokens: float32 [16384, 384], P(('replica', 'group'))
- grad_qkv: float32 [384, 1152], P(None, 'group')
- grad_out: float32 [384, 384], P(None, 'group')
- grad_up: float32 [384, 1536], P(None, 'group')
- grad_down: float32 [1536, 384], P('group')
- grad_vectors: float32 [12, 384], P(None, 'group')
- new_mom_qkv: float32 [384, 1152], P(None, 'group')
- new_mom_out: float32 [384, 384], P(None, 'group')
- new_mom_up: float32 [384, 1536], P(None, 'group')
- new_mom_down: float32 [1536, 384], P('group')
- new_mom_vectors: float32 [12, 384], P(None, 'group')
- update_qkv: float32 [384, 1152], P(None, 'group')
- update_out: float32 [384, 384], P(None, 'group')
- update_up: float32 [384, 1536], P(None, 'group')
- update_down: float32 [1536, 384], P('group')
- update_vectors: float32 [12, 384], P(None, 'group')
Inputs may be any that keep to these rules, and one draw needn't show every extreme that they name: Replica r holds images 0 to image_count[r] - 1 in its first 197 * image_count[r] slots; one replica holds 20 images and one holds 10.
All inputs are finite; a program needn't handle non-finite values.
Results may differ from a plain program's by a relative error of at most 0.0003.
Values sent between devices are 32-bit elements; how exact they have to be, the bound alone decides.
No kernel may reach another device: no remote copies, remote signals or barrier semaphores. Data moves between devices by JAX's collectives and lax.ppermute only.
A program may use at most 128 MiB of HBM per device.

v0:
```python
import jax
import jax.numpy as jnp
from jax import lax
from jax.sharding import PartitionSpec as P

D = 384
HEADS = 6
HEAD_DIM = 64
FF = 1536
L = 197
NS_STEPS = 5


precise = lax.Precision.HIGHEST
ns_coeffs = (3.4445, -4.775, 2.0315)
norm_eps = 1e-06
ns_eps = 1e-07
muon_momentum = 0.95
vector_momentum = 0.9
muon_rate = 0.5
vector_rate = 0.001
mask_fill = -1e30


def with_halo(cells, sides, width):
    for axis, dim in sides:
        count = lax.axis_size(axis)
        ends = count - 1
        head = lax.slice_in_dim(cells, 0, width, axis=dim)
        tail = lax.slice_in_dim(cells, cells.shape[dim] - width, cells.shape[dim], axis=dim)
        cells = jnp.concatenate(
            [
                lax.ppermute(tail, axis, [(i, (i + 1) % count) for i in range(ends)]),
                cells,
                lax.ppermute(head, axis, [((i + 1) % count, i) for i in range(ends)]),
            ],
            axis=dim,
        )
    return cells


def from_behind(x, axis, by):
    peers = lax.axis_size(axis)
    pairs = [(i, i + by) for i in range(peers) if 0 <= i + by < peers]
    return lax.ppermute(x, axis, pairs)


def matmul(left_side, right_side):
    return jnp.dot(left_side, right_side, precision=precise, preferred_element_type=jnp.float32)


def layer_norm(values, scale_delta, offset):
    centered = values - jnp.mean(values, axis=-1, keepdims=True)
    variance = jnp.mean(centered * centered, axis=-1, keepdims=True)
    return centered * lax.rsqrt(variance + norm_eps) * (1.0 + scale_delta) + offset


def newton_step(current, gram_mat):
    polynomial = ns_coeffs[1] * gram_mat + ns_coeffs[2] * matmul(gram_mat, gram_mat)
    return ns_coeffs[0] * current + matmul(polynomial, current)


def local(
    tokens,
    image_count,
    w_qkv,
    w_out,
    w_up,
    w_down,
    vectors,
    cotangent,
    mom_qkv,
    mom_out,
    mom_up,
    mom_down,
    mom_vectors,
):
    group_size = lax.axis_size("group")
    group_index = lax.axis_index("group")
    replica_index = lax.axis_index("replica")
    tok_rows = tokens.shape[0]
    margin = L - 1
    slab_rows = group_size * tok_rows
    image_runs = tok_rows // L + 2
    span_rows = image_runs * L
    extent = tok_rows + 2 * margin + 2 * L
    image_total = lax.dynamic_index_in_dim(image_count, replica_index, 0, keepdims=False)
    first_slot = group_index * tok_rows
    first_image = first_slot // L
    offset = first_image * L - first_slot + margin
    key_pos = first_slot - margin + offset + jnp.arange(span_rows, dtype=jnp.int32)
    key_keep = ((key_pos >= 0) & (key_pos < slab_rows)).reshape(image_runs, 1, 1, L)
    query_pos = first_slot + jnp.arange(tok_rows, dtype=jnp.int32)
    live_rows = (query_pos < image_total * L).astype(jnp.float32)[:, None]

    def image_blocks(queries, widened):
        query_pad = jnp.pad(queries, ((margin, extent - margin - tok_rows), (0, 0)))
        pair_pad = jnp.pad(widened, ((0, 0), (0, extent - tok_rows - 2 * margin), (0, 0)))
        block_q = lax.dynamic_slice_in_dim(query_pad, offset, span_rows, 0).reshape(
            image_runs, L, HEADS, HEAD_DIM
        )
        block_k = lax.dynamic_slice_in_dim(pair_pad[0], offset, span_rows, 0).reshape(
            image_runs, L, HEADS, HEAD_DIM
        )
        block_v = lax.dynamic_slice_in_dim(pair_pad[1], offset, span_rows, 0).reshape(
            image_runs, L, HEADS, HEAD_DIM
        )
        scores = jnp.einsum("sqhd,skhd->shqk", block_q, block_k, precision=precise) * HEAD_DIM ** (
            -0.5
        )
        scores = jnp.where(key_keep, scores, mask_fill)
        weights = jax.nn.softmax(scores, axis=-1)
        attended = jnp.einsum("shqk,skhd->sqhd", weights, block_v, precision=precise).reshape(
            span_rows, D
        )
        placed = lax.dynamic_update_slice_in_dim(
            jnp.zeros((extent, D), jnp.float32), attended, offset, 0
        )
        return placed[margin : margin + tok_rows]

    def project_part(qkv_whole, vectors_whole, inputs):
        normed = layer_norm(inputs, vectors_whole[0], vectors_whole[1])
        projected = matmul(normed, qkv_whole)
        queries = projected[:, :D] + vectors_whole[2]
        key_value = jnp.stack([projected[:, D : 2 * D], projected[:, 2 * D :] + vectors_whole[3]])
        return (queries, key_value)

    def rest_part(out_whole, up_whole, down_whole, vectors_whole, inputs, queries, widened):
        attended = image_blocks(queries, widened)
        middle = inputs + matmul(attended, out_whole) + vectors_whole[4]
        normed_two = layer_norm(middle, vectors_whole[5], vectors_whole[6])
        hidden = jax.nn.gelu(
            matmul(normed_two, up_whole) + vectors_whole[8:].reshape(FF), approximate=False
        )
        return middle + matmul(hidden, down_whole) + vectors_whole[7]

    whole = (
        lax.all_gather(w_qkv, "group", axis=1, tiled=True),
        lax.all_gather(w_out, "group", axis=1, tiled=True),
        lax.all_gather(w_up, "group", axis=1, tiled=True),
        lax.all_gather(w_down, "group", axis=0, tiled=True),
        lax.all_gather(vectors, "group", axis=1, tiled=True),
    )
    queries, key_value = project_part(whole[0], whole[4], tokens)
    widened = with_halo(key_value, (("group", 1),), margin)
    block_out = rest_part(whole[1], whole[2], whole[3], whole[4], tokens, queries, widened)
    second = (
        lax.all_gather(w_qkv, "group", axis=1, tiled=True),
        lax.all_gather(w_out, "group", axis=1, tiled=True),
        lax.all_gather(w_up, "group", axis=1, tiled=True),
        lax.all_gather(w_down, "group", axis=0, tiled=True),
        lax.all_gather(vectors, "group", axis=1, tiled=True),
    )
    masked = cotangent * live_rows
    unused_out, rest_back = jax.vjp(
        rest_part, second[1], second[2], second[3], second[4], tokens, queries, widened
    )
    (
        grad_out_full,
        grad_up_full,
        grad_down_full,
        grad_vec_rest,
        grad_tok_rest,
        grad_queries,
        grad_widened,
    ) = rest_back(masked)
    lower_rim = grad_widened[:, :margin]
    upper_rim = grad_widened[:, margin + tok_rows :]
    from_above = from_behind(lower_rim, "group", -1)
    from_below = from_behind(upper_rim, "group", 1)
    grad_pair = grad_widened[:, margin : margin + tok_rows]
    grad_pair = grad_pair.at[:, :margin].add(from_below).at[:, tok_rows - margin :].add(from_above)
    unused_project, project_back = jax.vjp(project_part, second[0], second[4], tokens)
    grad_qkv_full, grad_vec_project, grad_tok_project = project_back((grad_queries, grad_pair))
    grad_tokens = grad_tok_project + grad_tok_rest
    shares = (
        lax.psum_scatter(grad_qkv_full, "group", scatter_dimension=1, tiled=True),
        lax.psum_scatter(grad_out_full, "group", scatter_dimension=1, tiled=True),
        lax.psum_scatter(grad_up_full, "group", scatter_dimension=1, tiled=True),
        lax.psum_scatter(grad_down_full, "group", scatter_dimension=0, tiled=True),
        lax.psum_scatter(
            grad_vec_project + grad_vec_rest, "group", scatter_dimension=1, tiled=True
        ),
    )
    gradients = lax.psum((shares[0], shares[1], shares[2], shares[3], shares[4]), "replica")
    new_qkv = muon_momentum * mom_qkv + gradients[0]
    new_out = muon_momentum * mom_out + gradients[1]
    new_up = muon_momentum * mom_up + gradients[2]
    new_down = muon_momentum * mom_down + gradients[3]
    new_vectors = vector_momentum * mom_vectors + gradients[4]
    oriented = (new_qkv, new_out, new_up, new_down.T)
    totals = lax.psum(
        (
            jnp.sum(oriented[0] * oriented[0]),
            jnp.sum(oriented[1] * oriented[1]),
            jnp.sum(oriented[2] * oriented[2]),
            jnp.sum(oriented[3] * oriented[3]),
        ),
        "group",
    )
    current = tuple((oriented[member] / (jnp.sqrt(totals[member]) + ns_eps) for member in range(4)))
    for step_index in range(NS_STEPS):
        gram_sums = lax.psum(
            (
                matmul(current[0], current[0].T),
                matmul(current[1], current[1].T),
                matmul(current[2], current[2].T),
                matmul(current[3], current[3].T),
            ),
            "group",
        )
        current = tuple((newton_step(current[member], gram_sums[member]) for member in range(4)))
    update_qkv = -muon_rate * 3.0**0.5 * current[0]
    update_out = -muon_rate * current[1]
    update_up = -muon_rate * (FF / D) ** 0.5 * current[2]
    update_down = (-muon_rate * current[3]).T
    update_vectors = -vector_rate * new_vectors
    return (
        block_out,
        grad_tokens,
        gradients[0],
        gradients[1],
        gradients[2],
        gradients[3],
        gradients[4],
        new_qkv,
        new_out,
        new_up,
        new_down,
        new_vectors,
        update_qkv,
        update_out,
        update_up,
        update_down,
        update_vectors,
    )


def solution(mesh):
    return jax.shard_map(
        local,
        mesh=mesh,
        in_specs=(
            P(("replica", "group"), None),
            P(),
            P(None, "group"),
            P(None, "group"),
            P(None, "group"),
            P("group", None),
            P(None, "group"),
            P(("replica", "group"), None),
            P(None, "group"),
            P(None, "group"),
            P(None, "group"),
            P("group", None),
            P(None, "group"),
        ),
        out_specs=(
            P(("replica", "group"), None),
            P(("replica", "group"), None),
            P(None, "group"),
            P(None, "group"),
            P(None, "group"),
            P("group", None),
            P(None, "group"),
            P(None, "group"),
            P(None, "group"),
            P(None, "group"),
            P("group", None),
            P(None, "group"),
            P(None, "group"),
            P(None, "group"),
            P(None, "group"),
            P("group", None),
            P(None, "group"),
        ),
        check_vma=False,
    )
```

profile of v0, /device:TPU:0, one launch (start us, length us, event | category | flops | bytes accessed | tf_op | source)
XLA Modules:
  0.0 892.3 jit_solution(6600018434531862584)
XLA Ops:
  9.5 15.9 %all-gather = f32[8,48,12]{1,2,0:T(8,128)S(1)} all-gather(f32[1,48,12]{1,2,0:T(8,128)} %bitcast.197), channel_id=1, replica_groups=mesh['replica'=4,'group'=8] {'group'}, dimensions={0}, use_global_device_ids=true | all-gather | bytes 20736 | tf_op jit(solution)/shard_map/all_gather | solution.py:142
  30.3 8.6 all-gather.5.cloned.1.call-done
  38.9 8.1 fusion.53
  47.6 3.0 collective-permute-start
  53.0 35.2 %all_gather.22 = f32[384,384]{0,1:T(8,128)} all-gather(f32[384,48]{0,1:T(8,128)S(1)} %copy-done.58), channel_id=1, replica_groups=mesh['replica'=4,'group'=8] {'group'}, dimensions={1}, use_global_device_ids=true | all-gather | bytes 663552 | tf_op jit(solution)/shard_map/all_gather | solution.py:139
  89.5 3.3 reshape.282
  92.8 3.3 copy.83
  104.9 3.3 reshape.281
  108.2 3.2 copy.85
  111.4 6.5 fusion
  120.5 5.5 fusion.18
  126.0 3.6 copy.118
  129.6 3.5 reshape.274
  134.6 4.7 dynamic_update_slice.15
  142.3 17.0 %fusion.4 = (f32[512,1536]{1,0:T(8,128)}, f32[512,1536]{1,0:T(8,128)}) fusion(f32[1536]{0:T(1024)S(1)} %add.482, f32[384,1536]{0,1:T(8,128)} %all-gather.7.cloned.1.call-done, f32[512,384]{0,1:T(8,128)S(1)} %get-tuple-element.162, f32[384]{0:T(512)S(1)} %get-tuple-element.97, f32[384]{0:T(512)S(1)} %get-tuple-element.98, f32[512]{0:T(512)S(1)} %fusion.100, ...), kind=kOutput, calls=%fused_computation.19 | convolution fusion | flops 3674210304 | bytes 9450496 | tf_op jit(solution)/shard_map/dot_general | solution.py:49
  159.3 13.0 %fusion.125 = (f32[1536]{0:T(1024)}, f32[512,1536]{1,0:T(8,128)S(1)}) fusion(f32[512,1536]{1,0:T(8,128)} %get-tuple-element.163, f32[512,1536]{1,0:T(8,128)} %get-tuple-element.164, f32[1536,384]{1,0:T(8,128)} %all-gather.9.cloned.1.call-done, f32[512,384]{0,1:T(8,128)} %copy.91, f32[512]{0:T(512)S(1)} %fusion.98), kind=kOutput, calls=%fused_computation.262 | convolution fusion | flops 3635083776 | bytes 12591104 | tf_op jit(solution)/shard_map/transpose(jvp())/dot_general | solution.py:49
  172.3 6.5 fusion.124
  186.7 3.4 fusion.50
  190.2 8.5 fusion.54
  198.8 3.0 fusion.127
  203.1 3.3 reshape.275
  206.4 3.3 copy.94
  209.7 9.8 %fusion.19 = f32[4,197,6,64]{1,3,2,0:T(8,128)} fusion(f32[4,6,197]{2,1,0:T(8,128)S(1)} %fusion.89, f32[4,197,6,64]{1,3,2,0:T(8,128)} %copy.94, f32[4,6,197,197]{2,3,1,0:T(8,128)} %copy-done, f32[4,6,197]{2,1,0:T(8,128)S(1)} %get-tuple-element.159, pred[4,197]{1,0:T(4,128)(4,1)S(1)} %fusion.97), kind=kOutput, calls=%fused_computation.50 | convolution fusion | flops 719053184 | bytes 6185012 | tf_op jit(solution)/shard_map/transpose(jvp(shqk,skhd->sqhd))/dot_general | solution.py:113
  219.5 3.6 copy.121
  223.1 4.1 reshape.276
  227.2 13.2 %fusion.44 = f32[1536,384]{1,0:T(8,128)} fusion(f32[512,1536]{1,0:T(8,128)} %get-tuple-element.163, f32[512,1536]{1,0:T(8,128)} %get-tuple-element.164, f32[512,384]{0,1:T(8,128)} %copy.91, f32[512]{0:T(512)S(1)} %fusion.98), kind=kOutput, calls=%fused_computation.95 | convolution fusion | flops 3625648128 | bytes 9439232 | tf_op jit(solution)/shard_map/transpose(jvp())/dot_general | solution.py:49
  240.7 9.2 %multiply_reduce_fusion = (f32[4,6,197]{2,1,0:T(8,128)S(1)}, f32[4,6,197,197]{2,3,1,0:T(8,128)S(1)}) fusion(f32[4,6,197]{2,1,0:T(8,128)S(1)} %multiply_divide_fusion, f32[4,6,197]{2,1,0:T(8,128)S(1)} %get-tuple-element.159, f32[4,6,197,197]{2,3,1,0:T(8,128)} %copy-done, pred[4,197]{1,0:T(4,128)(4,1)S(1)} %fusion.97, f32[4,197,6,64]{1,3,2,0:T(8,128)} %copy.85, ...), kind=kOutput, calls=%fused_computation.1 | convolution fusion | flops 720911232 | bytes 9929588 | tf_op jit(solution)/shard_map/transpose(jvp(shqk,skhd->sqhd))/dot_general | solution.py:113
  249.9 3.7 select_multiply_fusion
  255.8 6.3 convolution_bitcast_fusion.1
  262.1 3.6 copy.122
  265.7 4.1 reshape.277
  285.1 4.9 convolution_bitcast_fusion
  290.0 3.6 copy.123
  293.5 3.5 reshape.278
  298.5 4.4 dynamic_update_slice.18
  309.9 5.4 fusion.12
  315.5 52.5 %reduce-scatter.8.cloned.1.call-done = f32[384,144]{0,1:T(8,128)} async-done(((f32[384,1152]{0,1:T(8,128)}), f32[384,144]{0,1:T(8,128)}) %reduce-scatter.8.cloned.1.call-update) | async-done | bytes 221200 | tf_op jit(solution)/shard_map/reduce_scatter | solution.py:177
  368.1 52.3 %all-reduce.41.cloned.1.call-done = (f32[384,144]{0,1:T(8,128)}, f32[384,48]{0,1:T(8,128)}, f32[384,192]{0,1:T(8,128)}, f32[192,384]{1,0:T(8,128)}) async-done(((f32[384,144]{0,1:T(8,128)}, f32[384,48]{0,1:T(8,128)}, f32[384,192]{0,1:T(8,128)}, f32[192,384]{1,0:T(8,128)}), (f32[384,144]{0,1:T(8,128)}, f32[384,48]{0,1:T(8,128)}, f32[384,192]{0,1:T(8,128)}, ...) | async-done | bytes 884752 | tf_op jit(solution)/shard_map/psum | solution.py:185
  427.1 17.2 %all-reduce.17 = (f32[]{:T(128)}, f32[]{:T(128)}, f32[]{:T(128)}, f32[]{:T(128)}) all-reduce(f32[]{:T(128)} %get-tuple-element.140, f32[]{:T(128)} %get-tuple-element.138, f32[]{:T(128)} %get-tuple-element.136, f32[]{:T(128)} %get-tuple-element.134), channel_id=1, replica_groups=mesh['replica'=4,'group'=8] {'group'}, use_global_device_ids=true, to_apply=%region_31.32 | all-reduce | flops 4 | bytes 32 | tf_op jit(solution)/shard_map/psum | solution.py:192
  453.7 64.6 %all-reduce.39.cloned.1.call-done = (f32[384,384]{1,0:T(8,128)}, f32[384,384]{1,0:T(8,128)}, f32[384,384]{1,0:T(8,128)}, f32[384,384]{1,0:T(8,128)}) async-done(((f32[384,384]{1,0:T(8,128)}, f32[384,384]{1,0:T(8,128)}, f32[384,384]{1,0:T(8,128)}, f32[384,384]{1,0:T(8,128)}), (f32[384,384]{1,0:T(8,128)}, f32[384,384]{1,0:T(8,128)}, f32[384,384]{1,0:T(8,128)}, ...) | async-done | bytes 2359312 | tf_op jit(solution)/shard_map/psum | solution.py:203
  535.3 66.0 %all-reduce.37.cloned.1.call-done = (f32[384,384]{1,0:T(8,128)}, f32[384,384]{1,0:T(8,128)}, f32[384,384]{1,0:T(8,128)}, f32[384,384]{1,0:T(8,128)}) async-done(((f32[384,384]{1,0:T(8,128)}, f32[384,384]{1,0:T(8,128)}, f32[384,384]{1,0:T(8,128)}, f32[384,384]{1,0:T(8,128)}), (f32[384,384]{1,0:T(8,128)}, f32[384,384]{1,0:T(8,128)}, f32[384,384]{1,0:T(8,128)}, ...) | async-done | bytes 2359312 | tf_op jit(solution)/shard_map/psum | solution.py:203
  618.7 66.3 %all-reduce.35.cloned.1.call-done = (f32[384,384]{1,0:T(8,128)}, f32[384,384]{1,0:T(8,128)}, f32[384,384]{1,0:T(8,128)}, f32[384,384]{1,0:T(8,128)}) async-done(((f32[384,384]{1,0:T(8,128)}, f32[384,384]{1,0:T(8,128)}, f32[384,384]{1,0:T(8,128)}, f32[384,384]{1,0:T(8,128)}), (f32[384,384]{1,0:T(8,128)}, f32[384,384]{1,0:T(8,128)}, f32[384,384]{1,0:T(8,128)}, ...) | async-done | bytes 2359312 | tf_op jit(solution)/shard_map/psum | solution.py:203
  705.1 8.0 fusion.126
  719.8 48.3 %all-reduce.33.cloned.1.call-done = (f32[384,384]{1,0:T(8,128)}, f32[384,384]{1,0:T(8,128)}, f32[384,384]{1,0:T(8,128)}, f32[384,384]{1,0:T(8,128)}) async-done(((f32[384,384]{1,0:T(8,128)}, f32[384,384]{1,0:T(8,128)}, f32[384,384]{1,0:T(8,128)}, f32[384,384]{1,0:T(8,128)}), (f32[384,384]{1,0:T(8,128)}, f32[384,384]{1,0:T(8,128)}, f32[384,384]{1,0:T(8,128)}, ...) | async-done | bytes 2359312 | tf_op jit(solution)/shard_map/psum | solution.py:203
  784.7 8.8 fusion.22
  797.3 3.3 reduce-scatter.16.cloned.1.call-done
  801.4 10.0 %psum.207 = f32[12,48]{1,0:T(8,128)S(1)} all-reduce(f32[12,48]{1,0:T(8,128)S(1)} %copy.125), channel_id=1, replica_groups=mesh['replica'=4,'group'=8] {'replica'}, use_global_device_ids=true, to_apply=%region_29.30 | all-reduce | flops 576 | bytes 4608 | tf_op jit(solution)/shard_map/psum | solution.py:185
  812.0 56.4 %all-reduce.31.cloned.1.call-done = (f32[384,384]{1,0:T(8,128)}, f32[384,384]{1,0:T(8,128)}, f32[384,384]{1,0:T(8,128)}, f32[384,384]{1,0:T(8,128)}) async-done(((f32[384,384]{1,0:T(8,128)}, f32[384,384]{1,0:T(8,128)}, f32[384,384]{1,0:T(8,128)}, f32[384,384]{1,0:T(8,128)}), (f32[384,384]{1,0:T(8,128)}, f32[384,384]{1,0:T(8,128)}, f32[384,384]{1,0:T(8,128)}, ...) | async-done | bytes 2359312 | tf_op jit(solution)/shard_map/psum | solution.py:203
  (332 shorter events, 174.5 us)
Async XLA Ops:
  7.2 20.4 %copy-start.18 = (f32[512,384]{1,0:T(8,128)S(1)}, f32[512,384]{1,0:T(8,128)}, u32[]{:S(2)}) copy-start(f32[512,384]{1,0:T(8,128)} %param.17) | copy-start | bytes 2359300
  7.2 20.7 %copy-start.45 = (f32[512,384]{1,0:T(8,128)S(1)}, f32[512,384]{1,0:T(8,128)}, u32[]{:S(2)}) copy-start(f32[512,384]{1,0:T(8,128)} %param.24) | copy-start | bytes 2359300
  7.2 21.9 %copy-start.71 = (s32[4]{0:T(128)S(1)}, s32[4]{0:T(128)}, u32[]{:S(2)}) copy-start(s32[4]{0:T(128)} %param.18) | copy-start | bytes 52
  7.2 31.7 %all-gather.5.cloned.1.call-start = ((), (), s32[]{:S(2)}) async-start(), calls=%async_computation.5 | async-start | bytes 1990656 | tf_op jit(solution)/shard_map/all_gather | solution.py:138
  8.0 134.3 %all-gather.7.cloned.1.call-start = ((), (), s32[]{:S(2)}) async-start(), calls=%async_computation.6 | async-start | bytes 2654208 | tf_op jit(solution)/shard_map/all_gather | solution.py:140
  8.7 150.6 %all-gather.9.cloned.1.call-start = ((), (), s32[]{:S(2)}) async-start(), calls=%async_computation.7 | async-start | bytes 2654208 | tf_op jit(solution)/shard_map/all_gather | solution.py:141
  9.4 306.0 %reduce-scatter.10.cloned.1.call-start = ((), (), s32[]{:S(2)}) async-start(), calls=%async_computation.9 | async-start | bytes 663552 | tf_op jit(solution)/shard_map/reduce_scatter | solution.py:178
  47.6 48.5 %collective-permute-start = (f32[2,196,384]{2,0,1:T(2,128)S(1)}, f32[2,196,384]{2,0,1:T(2,128)}, u32[]{:S(2)}, u32[]{:S(2)}) collective-permute-start(f32[2,196,384]{2,0,1:T(2,128)S(1)} %copy.76), channel_id=1, source_target_pairs={{0,1},{1,2},{2,3},{3,4},{4,5},{5,6},{6,7},{8,9},{9,10},{10,11},{11... | collective-permute-start | bytes 1806344 | tf_op jit(solution)/shard_map/ppermute | solution.py:33
  51.7 45.6 %collective-permute-start.1 = (f32[2,196,384]{2,0,1:T(2,128)}, f32[2,196,384]{2,0,1:T(2,128)}, u32[]{:S(2)}, u32[]{:S(2)}) collective-permute-start(f32[2,196,384]{2,0,1:T(2,128)} %copy.77), channel_id=1, source_target_pairs={{1,0},{2,1},{3,2},{4,3},{5,4},{6,5},{7,6},{9,8},{10,9},{11,10},{12... | collective-permute-start | bytes 1806344 | tf_op jit(solution)/shard_map/ppermute | solution.py:35
  159.3 13.0 %copy-start.23 = (f32[384,1536]{0,1:T(8,128)S(1)}, f32[384,1536]{0,1:T(8,128)}, u32[]{:S(2)}) copy-start(f32[384,1536]{0,1:T(8,128)} %all-gather.7.cloned.1.call-done) | copy-start | bytes 7077892
  190.1 125.3 %reduce-scatter.12.cloned.1.call-start = ((), (), s32[]{:S(2)}) async-start(), calls=%async_computation.10 | async-start | bytes 2654208 | tf_op jit(solution)/shard_map/reduce_scatter | solution.py:179
  198.7 116.7 %reduce-scatter.14.cloned.1.call-start = ((), (), s32[]{:S(2)}) async-start(), calls=%async_computation.11 | async-start | bytes 2654208 | tf_op jit(solution)/shard_map/reduce_scatter | solution.py:180
  240.5 127.5 %reduce-scatter.8.cloned.1.call-start = ((), (), s32[]{:S(2)}) async-start(), calls=%async_computation.8 | async-start | bytes 1990656 | tf_op jit(solution)/shard_map/reduce_scatter | solution.py:177
  275.5 9.5 %slice-start = ((s8[4915200]{0:T(1024)(128)(4,1)}), s8[4194304]{0:T(1024)(128)(4,1)S(1)}, s32[]{:S(2)}) async-start(s8[4915200]{0:T(1024)(128)(4,1)} %bitcast.187), calls=%async_computation.19 | async-start | bytes 8388608
  276.0 9.0 %slice-start.1 = ((s8[4915200]{0:T(1024)(128)(4,1)}), s8[720896]{0:T(1024)(128)(4,1)S(1)}, s32[]{:S(2)}) async-start(s8[4915200]{0:T(1024)(128)(4,1)} %bitcast.187), calls=%async_computation.20 | async-start | bytes 1441792
  276.0 4.2 collective-permute-start.2
  283.3 21.4 %collective-permute-start.3 = (f32[2,196,384]{2,0,1:T(2,128)}, f32[2,196,384]{2,0,1:T(2,128)}, u32[]{:S(2)}, u32[]{:S(2)}) collective-permute-start(f32[2,196,384]{2,0,1:T(2,128)} %get-tuple-element.146), channel_id=1, source_target_pairs={{1,0},{2,1},{3,2},{4,3},{5,4},{6,5},{7,6},{9,8},{10,9},{11,10},{12... | collective-permute-start | bytes 1806344 | tf_op jit(solution)/shard_map/ppermute | solution.py:45
  297.1 7.7 copy-start.8
  309.9 110.4 %copy-start.50 = (f32[192,384]{1,0:T(8,128)S(1)}, f32[192,384]{1,0:T(8,128)}, u32[]{:S(2)}) copy-start(f32[192,384]{1,0:T(8,128)} %param.28) | copy-start | bytes 884740
  315.3 106.7 %copy-start.51 = (f32[384,192]{0,1:T(8,128)S(1)}, f32[384,192]{0,1:T(8,128)}, u32[]{:S(2)}) copy-start(f32[384,192]{0,1:T(8,128)} %param.27) | copy-start | bytes 884740
  315.3 108.5 %copy-start.55 = (f32[384,144]{0,1:T(8,128)S(1)}, f32[384,144]{0,1:T(8,128)}, u32[]{:S(2)}) copy-start(f32[384,144]{0,1:T(8,128)} %param.25) | copy-start | bytes 663556
  315.3 110.2 %copy-start.57 = (f32[384,48]{0,1:T(8,128)S(1)}, f32[384,48]{0,1:T(8,128)}, u32[]{:S(2)}) copy-start(f32[384,48]{0,1:T(8,128)} %param.26) | copy-start | bytes 221188
  315.4 105.0 %all-reduce.41.cloned.1.call-start = ((), (), s32[]{:S(2)}) async-start(), calls=%async_computation.18 | async-start | bytes 1769472 | tf_op jit(solution)/shard_map/psum | solution.py:185
  368.0 150.3 %all-reduce.39.cloned.1.call-start = ((), (), s32[]{:S(2)}) async-start(), calls=%async_computation.17 | async-start | bytes 4718592 | tf_op jit(solution)/shard_map/psum | solution.py:203
  422.1 182.1 %copy-start.19 = (f32[192,384]{1,0:T(8,128)}, f32[192,384]{1,0:T(8,128)S(1)}, u32[]{:S(2)}) copy-start(f32[192,384]{1,0:T(8,128)S(1)} %get-tuple-element.187) | copy-start | bytes 884740
  423.8 101.1 %copy-start.52 = (f32[384,192]{0,1:T(8,128)}, f32[384,192]{0,1:T(8,128)S(1)}, u32[]{:S(2)}) copy-start(f32[384,192]{0,1:T(8,128)S(1)} %get-tuple-element.186) | copy-start | bytes 884740
  425.5 106.8 %copy-start.56 = (f32[384,144]{0,1:T(8,128)}, f32[384,144]{0,1:T(8,128)S(1)}, u32[]{:S(2)}) copy-start(f32[384,144]{0,1:T(8,128)S(1)} %get-tuple-element.184) | copy-start | bytes 663556
  427.1 101.7 %copy-start.49 = (f32[384,48]{0,1:T(8,128)}, f32[384,48]{0,1:T(8,128)S(1)}, u32[]{:S(2)}) copy-start(f32[384,48]{0,1:T(8,128)S(1)} %get-tuple-element.185) | copy-start | bytes 221188
  453.6 147.6 %all-reduce.37.cloned.1.call-start = ((), (), s32[]{:S(2)}) async-start(), calls=%async_computation.16 | async-start | bytes 4718592 | tf_op jit(solution)/shard_map/psum | solution.py:203
  521.9 82.2 %copy-start.42 = (f32[384,192]{0,1:T(8,128)}, f32[384,192]{0,1:T(8,128)S(1)}, u32[]{:S(2)}) copy-start(f32[384,192]{0,1:T(8,128)S(1)} %fusion.119) | copy-start | bytes 884740
  534.8 150.2 %all-reduce.35.cloned.1.call-start = ((), (), s32[]{:S(2)}) async-start(), calls=%async_computation.15 | async-start | bytes 4718592 | tf_op jit(solution)/shard_map/psum | solution.py:203
  618.5 149.6 %all-reduce.33.cloned.1.call-start = ((), (), s32[]{:S(2)}) async-start(), calls=%async_computation.14 | async-start | bytes 4718592 | tf_op jit(solution)/shard_map/psum | solution.py:203
  688.6 83.1 %copy-start.9 = (f32[384,192]{0,1:T(8,128)}, f32[384,192]{0,1:T(8,128)S(1)}, u32[]{:S(2)}) copy-start(f32[384,192]{0,1:T(8,128)S(1)} %fusion.141) | copy-start | bytes 884740
  701.6 99.0 %reduce-scatter.16.cloned.1.call-start = ((), (), s32[]{:S(2)}) async-start(), calls=%async_computation.12 | async-start | bytes 221184
  719.3 149.1 %all-reduce.31.cloned.1.call-start = ((), (), s32[]{:S(2)}) async-start(), calls=%async_computation.13 | async-start | bytes 4718592 | tf_op jit(solution)/shard_map/psum | solution.py:203
  784.7 11.1 %copy-start.6 = (f32[512,384]{0,1:T(8,128)S(1)}, f32[512,384]{0,1:T(8,128)}, u32[]{:S(2)}) copy-start(f32[512,384]{0,1:T(8,128)} %copy-done.5) | copy-start | bytes 2359300
  784.7 11.1 %copy-start.61 = (f32[512]{0:T(512)S(1)}, f32[512]{0:T(512)}, u32[]{:S(2)}) copy-start(f32[512]{0:T(512)} %copy-done.60) | copy-start | bytes 6148
  793.5 17.8 %copy-start.68 = (f32[12,48]{1,0:T(8,128)S(1)}, f32[12,48]{1,0:T(8,128)}, u32[]{:S(2)}) copy-start(f32[12,48]{1,0:T(8,128)} %param.29) | copy-start | bytes 6916
  796.1 78.1 %copy-start.15 = (f32[384,192]{0,1:T(8,128)S(1)}, f32[384,192]{0,1:T(8,128)}, u32[]{:S(2)}) copy-start(f32[384,192]{0,1:T(8,128)} %copy-done.14) | copy-start | bytes 884740
  811.4 65.7 %copy-start.59 = (f32[12,48]{1,0:T(8,128)}, f32[12,48]{1,0:T(8,128)S(1)}, u32[]{:S(2)}) copy-start(f32[12,48]{1,0:T(8,128)S(1)} %psum.207) | copy-start | bytes 6916
  868.4 7.4 copy-start.28
  868.4 8.7 copy-start.39
  871.4 7.1 copy-start.27
  874.2 7.0 copy-start.10
  874.2 7.0 copy-start.20
  874.2 7.0 copy-start.22
  874.3 7.0 copy-start.43
  874.3 7.0 copy-start.54
  (44 other events, 200.1 us)
Sparse Core Ops, SparseCore 0:
  9.7 29.1 all-gather.4
  40.5 35.3 all-gather.6
  77.6 34.0 all-gather.8
  190.3 29.5 reduce-scatter.9
  222.0 34.4 reduce-scatter.11
  258.6 38.3 reduce-scatter.13
  315.5 52.4 reduce-scatter.7
  371.4 48.9 all-reduce.40
  453.7 64.5 all-reduce.38
  534.9 66.2 all-reduce.36
  618.6 66.3 all-reduce.34
  701.7 66.3 all-reduce.32
  771.0 29.5 reduce-scatter.15
  803.1 65.3 all-reduce.30
where the time goes:
time: 901 us; the launch traced here: 892 us
  waiting for transfers between devices  421 us (47%)
  matrix products  227 us (25%)
  local copies, waits for them, and re-layouts  107 us (12%)
  blocking collectives  78.3 us (9%)
  other arithmetic  30.2 us (3%)
  between operations  18.8 us (2%)
  starting transfers between devices  10.2 us (1%)
    psum x5, waiting for transfers between devices, local(): lax.psum((matmul(current[0], current[0].T), matmul(current[1], current[1]...  302 us
    dot_general x72, matrix products, matmul(): jnp.dot(left_side, right_side, precision=precise, preferred_element_type=...  185 us
    reduce_scatter x1, waiting for transfers between devices, local(): lax.psum_scatter(grad_qkv_full, 'group', scatter_dimension=1, tiled=True)  52.5 us
    psum x1, waiting for transfers between devices, local(): lax.psum((shares[0], shares[1], shares[2], shares[3], shares[4]), 'replica')  52.3 us
    all_gather x1, blocking collectives, local(): lax.all_gather(w_out, 'group', axis=1, tiled=True)  35.2 us
    dot_general x3, matrix products, image_blocks(): jnp.einsum('shqk,skhd->sqhd', weights, block_v, precision=precise)  24.5 us
    unnamed x161, local copies, waits for them, and re-layouts  18.8 us
  transfers between devices with their start and end apart: 18, of which 10 were waited for; matrix products, arithmetic and copies ran while one was open for 28% of the time, Pallas kernels for 0%

commit v1 on v0

--- a/solution.py
+++ b/solution.py
@@ -55,9 +55,15 @@
     return centered * lax.rsqrt(variance + norm_eps) * (1.0 + scale_delta) + offset
 
 
-def newton_step(current, gram_mat):
-    polynomial = ns_coeffs[1] * gram_mat + ns_coeffs[2] * matmul(gram_mat, gram_mat)
-    return ns_coeffs[0] * current + matmul(polynomial, current)
+def polar_factor(gram_mat, block):
+    factor = None
+    for step_index in range(NS_STEPS):
+        square = matmul(gram_mat, gram_mat)
+        poly = ns_coeffs[1] * gram_mat + ns_coeffs[2] * square + ns_coeffs[0] * jnp.eye(D, dtype=jnp.float32)
+        factor = poly if factor is None else matmul(poly, factor)
+        if step_index + 1 < NS_STEPS:
+            gram_mat = matmul(poly, matmul(gram_mat, poly))
+    return matmul(factor, block)
 
 
 def local(
@@ -144,13 +150,7 @@
     queries, key_value = project_part(whole[0], whole[4], tokens)
     widened = with_halo(key_value, (("group", 1),), margin)
     block_out = rest_part(whole[1], whole[2], whole[3], whole[4], tokens, queries, widened)
-    second = (
-        lax.all_gather(w_qkv, "group", axis=1, tiled=True),
-        lax.all_gather(w_out, "group", axis=1, tiled=True),
-        lax.all_gather(w_up, "group", axis=1, tiled=True),
-        lax.all_gather(w_down, "group", axis=0, tiled=True),
-        lax.all_gather(vectors, "group", axis=1, tiled=True),
-    )
+    second = whole
     masked = cotangent * live_rows
     unused_out, rest_back = jax.vjp(
         rest_part, second[1], second[2], second[3], second[4], tokens, queries, widened
@@ -199,17 +199,8 @@
         "group",
     )
     current = tuple((oriented[member] / (jnp.sqrt(totals[member]) + ns_eps) for member in range(4)))
-    for step_index in range(NS_STEPS):
-        gram_sums = lax.psum(
-            (
-                matmul(current[0], current[0].T),
-                matmul(current[1], current[1].T),
-                matmul(current[2], current[2].T),
-                matmul(current[3], current[3].T),
-            ),
-            "group",
-        )
-        current = tuple((newton_step(current[member], gram_sums[member]) for member in range(4)))
+    gram_sums = lax.psum(tuple(matmul(member, member.T) for member in current), "group")
+    current = tuple(polar_factor(gram_sums[member], current[member]) for member in range(4))
     update_qkv = -muon_rate * 3.0**0.5 * current[0]
     update_out = -muon_rate * current[1]
     update_up = -muon_rate * (FF / D) ** 0.5 * current[2]

time: 901 us -> 634 us (0.70)
  waiting for transfers between devices: 421 us -> 150 us
  matrix products: 227 us -> 241 us
    psum x5 -> x1, waiting for transfers between devices: 302 us -> 42.9 us  [local(): lax.psum(tuple((matmul(member, member.T) for member in current)), 'group')]
    dot_general x72 -> x88, matrix products: 185 us -> 199 us  [matmul(): jnp.dot(left_side, right_side, precision=precise, preferred_element_type=...]
    psum x1, waiting for transfers between devices: 52.3 us -> 42.6 us  [local(): lax.psum((shares[0], shares[1], shares[2], shares[3], shares[4]), 'replica')]
    unnamed x161 -> x93, local copies, waits for them, and re-layouts: 18.8 us -> 17.3 us
  transfers between devices with their start and end apart: 18 -> 14, of which waited for: 10 -> 5; matrix products, arithmetic and copies ran while one was open for 28% -> 38% of each run, Pallas kernels for 0% -> 0%
where the time goes in v1:
time: 634 us; the launch traced here: 625 us
  matrix products  241 us (38%)
  waiting for transfers between devices  150 us (24%)
  local copies, waits for them, and re-layouts  101 us (16%)
  blocking collectives  77.6 us (12%)
  other arithmetic  26.6 us (4%)
  between operations  19.2 us (3%)
  starting transfers between devices  9.26 us (1%)
    dot_general x88, matrix products, matmul(): jnp.dot(left_side, right_side, precision=precise, preferred_element_type=...  199 us
    reduce_scatter x1, waiting for transfers between devices, local(): lax.psum_scatter(grad_qkv_full, 'group', scatter_dimension=1, tiled=True)  52.5 us
    psum x1, waiting for transfers between devices, local(): lax.psum(tuple((matmul(member, member.T) for member in current)), 'group')  42.9 us
    psum x1, waiting for transfers between devices, local(): lax.psum((shares[0], shares[1], shares[2], shares[3], shares[4]), 'replica')  42.6 us
    all_gather x1, blocking collectives, local(): lax.all_gather(w_out, 'group', axis=1, tiled=True)  35.2 us
    dot_general x3, matrix products, image_blocks(): jnp.einsum('shqk,skhd->sqhd', weights, block_v, precision=precise)  24.6 us
    dot_general x3, matrix products, image_blocks(): jnp.einsum('sqhd,skhd->shqk', block_q, block_k, precision=precise)  17.7 us
    unnamed x93, local copies, waits for them, and re-layouts  17.3 us
  transfers between devices with their start and end apart: 14, of which 5 were waited for; matrix products, arithmetic and copies ran while one was open for 38% of the time, Pallas kernels for 0%

profile of v1, /device:TPU:0, one launch (start us, length us, event | category | flops | bytes accessed | tf_op | source)
XLA Modules:
  0.0 625.1 jit_solution(15573310409100291906)
XLA Ops:
  9.5 15.9 %all-gather = f32[8,48,12]{1,2,0:T(8,128)S(1)} all-gather(f32[1,48,12]{1,2,0:T(8,128)} %bitcast.206), channel_id=1, replica_groups=mesh['replica'=4,'group'=8] {'group'}, dimensions={0}, use_global_device_ids=true | all-gather | bytes 20736 | tf_op jit(solution)/shard_map/all_gather | solution.py:148
  29.8 9.1 %all-gather.5.cloned.1.call-done = f32[384,1152]{0,1:T(8,128)} async-done(((f32[384,144]{0,1:T(8,128)}), f32[384,1152]{0,1:T(8,128)}) %all-gather.5.cloned.1.call-update) | async-done | bytes 1769488 | tf_op jit(solution)/shard_map/all_gather | solution.py:144
  38.9 8.1 %fusion.49 = f32[512,1152]{1,0:T(8,128)S(1)} fusion(f32[384,1152]{0,1:T(8,128)} %all-gather.5.cloned.1.call-done, f32[512,384]{0,1:T(8,128)S(1)} %copy.89, f32[384]{0:T(512)S(1)} %get-tuple-element.102, f32[384]{0:T(512)S(1)} %get-tuple-element.103, f32[512]{0:T(512)S(1)} %fusion.89, f32[512]{0:T(512)S(1)} %broadcast_multiply_fusion.2), kind=kOutput, calls=%fused_computation.141 | convolution fusion | flops 2718695424 | bytes 4922368 | tf_op jit(solution)/shard_map/dot_general | solution.py:49
  47.6 3.0 collective-permute-start
  53.0 35.2 %all_gather.17 = f32[384,384]{0,1:T(8,128)} all-gather(f32[384,48]{0,1:T(8,128)S(1)} %copy-done.34), channel_id=1, replica_groups=mesh['replica'=4,'group'=8] {'group'}, dimensions={1}, use_global_device_ids=true | all-gather | bytes 663552 | tf_op jit(solution)/shard_map/all_gather | solution.py:145
  89.5 3.3 reshape.282
  92.8 3.3 copy.83
  102.5 2.4 copy.84
  104.9 3.3 reshape.281
  108.2 3.3 copy.85
  111.6 6.5 %fusion = (f32[4,6,197]{2,1,0:T(8,128)S(1)}, f32[4,6,197,197]{2,3,1,0:T(8,128)S(1)}) fusion(pred[4,197]{1,0:T(4,128)(4,1)S(1)} %fusion.87, f32[4,197,6,64]{1,3,2,0:T(8,128)} %copy.83, f32[4,197,6,64]{1,3,2,0:T(8,128)S(1)} %copy.84), kind=kOutput, calls=%fused_computation.5 | convolution fusion | flops 718116992 | bytes 6166100 | tf_op jit(solution)/shard_map/sqhd,skhd->shqk/dot_general | solution.py:114
  120.6 5.5 fusion.18
  126.2 3.6 copy.118
  129.7 3.5 reshape.274
  134.7 4.7 dynamic_update_slice.15
  139.4 2.8 fusion.105
  142.4 17.0 %fusion.4 = (f32[512,1536]{1,0:T(8,128)}, f32[512,1536]{1,0:T(8,128)}) fusion(f32[1536]{0:T(1024)S(1)} %add.437, f32[384,1536]{0,1:T(8,128)} %all-gather.7.cloned.1.call-done, f32[512,384]{0,1:T(8,128)S(1)} %get-tuple-element.146, f32[384]{0:T(512)S(1)} %get-tuple-element.97, f32[384]{0:T(512)S(1)} %get-tuple-element.98, f32[512]{0:T(512)S(1)} %fusion.90, ...), kind=kOutput, calls=%fused_computation.39 | convolution fusion | flops 3674210304 | bytes 9450496 | tf_op jit(solution)/shard_map/dot_general | solution.py:49
  159.4 12.4 %fusion.107 = (f32[1536]{0:T(1024)S(1)}, f32[512,1536]{1,0:T(8,128)S(1)}) fusion(f32[512,1536]{1,0:T(8,128)} %get-tuple-element.147, f32[512,1536]{1,0:T(8,128)} %get-tuple-element.148, f32[1536,384]{1,0:T(8,128)} %all-gather.9.cloned.1.call-done, f32[512,384]{0,1:T(8,128)} %copy.91, f32[512]{0:T(512)S(1)} %fusion.88), kind=kOutput, calls=%fused_computation.245 | convolution fusion | flops 3635083776 | bytes 12591104 | tf_op jit(solution)/shard_map/transpose(jvp())/dot_general | solution.py:49
  171.9 6.0 fusion.106
  184.5 3.5 fusion.46
  188.0 8.6 %fusion.50 = f32[384,1536]{0,1:T(8,128)} fusion(f32[512,1536]{1,0:T(8,128)} %copy-done.3, f32[512,384]{0,1:T(8,128)S(1)} %get-tuple-element.146, f32[384]{0:T(512)S(1)} %get-tuple-element.97, f32[384]{0:T(512)S(1)} %get-tuple-element.98, f32[512]{0:T(512)S(1)} %fusion.90, f32[512]{0:T(512)S(1)} %broadcast_multiply_fusion.1), kind=kOutput, calls=%fused_computation.142 | convolution fusion | flops 3624665088 | bytes 6298624 | tf_op jit(solution)/shard_map/transpose(jvp())/dot_general | solution.py:49
  196.7 3.0 fusion.109
  201.0 3.3 reshape.275
  204.3 3.3 copy.94
  207.5 9.9 %fusion.19 = f32[4,197,6,64]{1,3,2,0:T(8,128)} fusion(f32[4,6,197]{2,1,0:T(8,128)S(1)} %fusion.80, f32[4,197,6,64]{1,3,2,0:T(8,128)} %copy.94, f32[4,6,197,197]{2,3,1,0:T(8,128)} %copy-done, f32[4,6,197]{2,1,0:T(8,128)S(1)} %get-tuple-element.143, pred[4,197]{1,0:T(4,128)(4,1)S(1)} %fusion.87), kind=kOutput, calls=%fused_computation.70 | convolution fusion | flops 719053184 | bytes 6185012 | tf_op jit(solution)/shard_map/transpose(jvp(shqk,skhd->sqhd))/dot_general | solution.py:119
  217.4 3.6 copy.121
  221.0 4.1 reshape.276
  225.1 13.2 %fusion.44 = f32[1536,384]{1,0:T(8,128)} fusion(f32[512,1536]{1,0:T(8,128)} %get-tuple-element.147, f32[512,1536]{1,0:T(8,128)} %get-tuple-element.148, f32[512,384]{0,1:T(8,128)} %copy.91, f32[512]{0:T(512)S(1)} %fusion.88), kind=kOutput, calls=%fused_computation.115 | convolution fusion | flops 3625648128 | bytes 9439232 | tf_op jit(solution)/shard_map/transpose(jvp())/dot_general | solution.py:49
  238.6 9.2 %multiply_reduce_fusion = (f32[4,6,197]{2,1,0:T(8,128)S(1)}, f32[4,6,197,197]{2,3,1,0:T(8,128)S(1)}) fusion(f32[4,6,197]{2,1,0:T(8,128)S(1)} %multiply_divide_fusion, f32[4,6,197]{2,1,0:T(8,128)S(1)} %get-tuple-element.143, f32[4,6,197,197]{2,3,1,0:T(8,128)} %copy-done, pred[4,197]{1,0:T(4,128)(4,1)S(1)} %fusion.87, f32[4,197,6,64]{1,3,2,0:T(8,128)} %copy.85, ...), kind=kOutput, calls=%fused_computation.1 | convolution fusion | flops 720911232 | bytes 9929588 | tf_op jit(solution)/shard_map/transpose(jvp(shqk,skhd->sqhd))/dot_general | solution.py:119
  247.8 3.7 select_multiply_fusion
  253.6 6.3 %convolution_bitcast_fusion.1 = f32[4,197,6,64]{1,3,2,0:T(8,128)} fusion(f32[4,6,197,197]{2,3,1,0:T(8,128)S(1)} %select_multiply_fusion, f32[4,197,6,64]{1,3,2,0:T(8,128)S(1)} %copy-done.2), kind=kOutput, calls=%fused_computation.68 | convolution fusion | flops 715327488 | bytes 6146400 | tf_op jit(solution)/shard_map/transpose(jvp(sqhd,skhd->shqk))/dot_general | solution.py:114
  259.9 3.6 copy.122
  263.5 4.1 reshape.277
  273.9 2.6 collective-permute-start.2
  282.8 4.9 convolution_bitcast_fusion
  287.7 3.6 copy.123
  291.3 3.5 reshape.278
  296.3 4.4 dynamic_update_slice.18
  306.6 5.4 fusion.12
  312.2 52.5 %reduce-scatter.8.cloned.1.call-done = f32[384,144]{0,1:T(8,128)} async-done(((f32[384,1152]{0,1:T(8,128)}), f32[384,144]{0,1:T(8,128)}) %reduce-scatter.8.cloned.1.call-update) | async-done | bytes 221200 | tf_op jit(solution)/shard_map/reduce_scatter | solution.py:177
  365.0 6.6 %fusion.108 = (f32[384]{0:T(512)S(1)}, f32[512,384]{1,0:T(8,128)}) fusion(f32[384,1152]{0,1:T(8,128)S(1)} %copy-done.17, f32[512,384]{1,0:T(8,128)} %copy-done.23, f32[512,384]{1,0:T(8,128)} %bitcast.201, f32[512,384]{1,0:T(8,128)} %bitcast.199), kind=kOutput, calls=%fused_computation.246 | convolution fusion | flops 2719284736 | bytes 4916736 | tf_op jit(solution)/shard_map/transpose(jvp())/dot_general | solution.py:49
  374.6 42.6 %all-reduce.25.cloned.1.call-done = (f32[384,144]{0,1:T(8,128)}, f32[384,48]{0,1:T(8,128)}, f32[384,192]{0,1:T(8,128)}, f32[192,384]{1,0:T(8,128)}) async-done(((f32[384,144]{0,1:T(8,128)}, f32[384,48]{0,1:T(8,128)}, f32[384,192]{0,1:T(8,128)}, f32[192,384]{1,0:T(8,128)}), (f32[384,144]{0,1:T(8,128)}, f32[384,48]{0,1:T(8,128)}, f32[384,192]{0,1:T(8,128)}, ...) | async-done | bytes 884752 | tf_op jit(solution)/shard_map/psum | solution.py:185
  424.6 17.0 %all-reduce.17 = (f32[]{:T(128)}, f32[]{:T(128)}, f32[]{:T(128)}, f32[]{:T(128)}) all-reduce(f32[]{:T(128)} %get-tuple-element.124, f32[]{:T(128)} %get-tuple-element.122, f32[]{:T(128)} %get-tuple-element.120, f32[]{:T(128)} %get-tuple-element.118), channel_id=1, replica_groups=mesh['replica'=4,'group'=8] {'group'}, use_global_device_ids=true, to_apply=%region_31.32 | all-reduce | flops 4 | bytes 32 | tf_op jit(solution)/shard_map/psum | solution.py:192
  444.3 2.8 fusion.82
  452.1 8.6 %fusion.22 = f32[512,384]{0,1:T(8,128)} fusion(f32[512,384]{0,1:T(8,128)S(1)} %get-tuple-element.146, f32[1536,384]{1,0:T(8,128)} %all-gather.9.cloned.1.call-done, f32[512,1536]{1,0:T(8,128)} %get-tuple-element.147, f32[512,1536]{1,0:T(8,128)} %get-tuple-element.148, f32[384]{0:T(512)S(1)} %get-tuple-element.96), kind=kOutput, calls=%fused_computation.72 | convolution fusion | flops 3625844736 | bytes 10225152 | tf_op jit(solution)/shard_map/dot_general | solution.py:49
  465.2 9.5 %psum.95 = f32[12,48]{1,0:T(8,128)S(1)} all-reduce(f32[12,48]{1,0:T(8,128)S(1)} %copy.125), channel_id=1, replica_groups=mesh['replica'=4,'group'=8] {'replica'}, use_global_device_ids=true, to_apply=%region_29.30 | all-reduce | flops 576 | bytes 4608 | tf_op jit(solution)/shard_map/psum | solution.py:185
  475.4 42.9 %all-reduce.23.cloned.1.call-done = (f32[384,384]{1,0:T(8,128)}, f32[384,384]{1,0:T(8,128)}, f32[384,384]{1,0:T(8,128)}, f32[384,384]{1,0:T(8,128)}) async-done(((f32[384,384]{1,0:T(8,128)}, f32[384,384]{1,0:T(8,128)}, f32[384,384]{1,0:T(8,128)}, f32[384,384]{1,0:T(8,128)}), (f32[384,384]{1,0:T(8,128)}, f32[384,384]{1,0:T(8,128)}, f32[384,384]{1,0:T(8,128)}, ...) | async-done | bytes 2359312 | tf_op jit(solution)/shard_map/psum | solution.py:202
  518.2 2.8 select_add_fusion.4
  (268 shorter events, 168.0 us)
Async XLA Ops:
  7.2 19.8 %copy-start.15 = (f32[512,384]{1,0:T(8,128)S(1)}, f32[512,384]{1,0:T(8,128)}, u32[]{:S(2)}) copy-start(f32[512,384]{1,0:T(8,128)} %param.17) | copy-start | bytes 2359300
  7.2 20.2 %copy-start.22 = (f32[512,384]{1,0:T(8,128)S(1)}, f32[512,384]{1,0:T(8,128)}, u32[]{:S(2)}) copy-start(f32[512,384]{1,0:T(8,128)} %param.24) | copy-start | bytes 2359300
  7.2 21.3 %copy-start.37 = (s32[4]{0:T(128)S(1)}, s32[4]{0:T(128)}, u32[]{:S(2)}) copy-start(s32[4]{0:T(128)} %param.18) | copy-start | bytes 52
  7.2 31.7 %all-gather.5.cloned.1.call-start = ((), (), s32[]{:S(2)}) async-start(), calls=%async_computation.5 | async-start | bytes 1990656 | tf_op jit(solution)/shard_map/all_gather | solution.py:144
  8.0 134.4 %all-gather.7.cloned.1.call-start = ((), (), s32[]{:S(2)}) async-start(), calls=%async_computation.6 | async-start | bytes 2654208 | tf_op jit(solution)/shard_map/all_gather | solution.py:146
  8.7 150.7 %all-gather.9.cloned.1.call-start = ((), (), s32[]{:S(2)}) async-start(), calls=%async_computation.7 | async-start | bytes 2654208 | tf_op jit(solution)/shard_map/all_gather | solution.py:147
  9.4 302.7 %reduce-scatter.10.cloned.1.call-start = ((), (), s32[]{:S(2)}) async-start(), calls=%async_computation.9 | async-start | bytes 663552 | tf_op jit(solution)/shard_map/reduce_scatter | solution.py:178
  47.2 5.8 copy-start.34
  47.6 48.5 %collective-permute-start = (f32[2,196,384]{2,0,1:T(2,128)S(1)}, f32[2,196,384]{2,0,1:T(2,128)}, u32[]{:S(2)}, u32[]{:S(2)}) collective-permute-start(f32[2,196,384]{2,0,1:T(2,128)S(1)} %copy.76), channel_id=1, source_target_pairs={{0,1},{1,2},{2,3},{3,4},{4,5},{5,6},{6,7},{8,9},{9,10},{10,11},{11... | collective-permute-start | bytes 1806344 | tf_op jit(solution)/shard_map/ppermute | solution.py:33
  51.7 45.5 %collective-permute-start.1 = (f32[2,196,384]{2,0,1:T(2,128)}, f32[2,196,384]{2,0,1:T(2,128)}, u32[]{:S(2)}, u32[]{:S(2)}) collective-permute-start(f32[2,196,384]{2,0,1:T(2,128)} %copy.77), channel_id=1, source_target_pairs={{1,0},{2,1},{3,2},{4,3},{5,4},{6,5},{7,6},{9,8},{10,9},{11,10},{12... | collective-permute-start | bytes 1806344 | tf_op jit(solution)/shard_map/ppermute | solution.py:35
  118.1 2.6 copy-start.10
  159.4 12.5 %copy-start.16 = (f32[384,1536]{0,1:T(8,128)S(1)}, f32[384,1536]{0,1:T(8,128)}, u32[]{:S(2)}) copy-start(f32[384,1536]{0,1:T(8,128)} %all-gather.7.cloned.1.call-done) | copy-start | bytes 7077892
  171.8 6.0 copy-start.3
  180.1 2.9 copy-start.4
  180.1 2.9 copy-start.9
  188.0 124.2 %reduce-scatter.12.cloned.1.call-start = ((), (), s32[]{:S(2)}) async-start(), calls=%async_computation.10 | async-start | bytes 2654208 | tf_op jit(solution)/shard_map/reduce_scatter | solution.py:179
  196.6 115.6 %reduce-scatter.14.cloned.1.call-start = ((), (), s32[]{:S(2)}) async-start(), calls=%async_computation.11 | async-start | bytes 2654208 | tf_op jit(solution)/shard_map/reduce_scatter | solution.py:180
  238.4 126.4 %reduce-scatter.8.cloned.1.call-start = ((), (), s32[]{:S(2)}) async-start(), calls=%async_computation.8 | async-start | bytes 1990656 | tf_op jit(solution)/shard_map/reduce_scatter | solution.py:177
  247.8 5.9 copy-start.2
  267.6 4.6 copy-start.14
  273.4 9.5 %slice-start = ((s8[4915200]{0:T(1024)(128)(4,1)}), s8[4194304]{0:T(1024)(128)(4,1)S(1)}, s32[]{:S(2)}) async-start(s8[4915200]{0:T(1024)(128)(4,1)} %bitcast.196), calls=%async_computation.15 | async-start | bytes 8388608
  273.8 9.0 %slice-start.1 = ((s8[4915200]{0:T(1024)(128)(4,1)}), s8[720896]{0:T(1024)(128)(4,1)S(1)}, s32[]{:S(2)}) async-start(s8[4915200]{0:T(1024)(128)(4,1)} %bitcast.196), calls=%async_computation.16 | async-start | bytes 1441792
  273.9 4.2 collective-permute-start.2
  281.1 20.8 %collective-permute-start.3 = (f32[2,196,384]{2,0,1:T(2,128)}, f32[2,196,384]{2,0,1:T(2,128)}, u32[]{:S(2)}, u32[]{:S(2)}) collective-permute-start(f32[2,196,384]{2,0,1:T(2,128)} %get-tuple-element.130), channel_id=1, source_target_pairs={{1,0},{2,1},{3,2},{4,3},{5,4},{6,5},{7,6},{9,8},{10,9},{11,10},{12... | collective-permute-start | bytes 1806344 | tf_op jit(solution)/shard_map/ppermute | solution.py:45
  294.9 7.1 %copy-start.8 = (f32[2,512,384]{2,0,1:T(2,128)S(1)}, f32[2,512,384]{2,0,1:T(2,128)}, u32[]{:S(2)}) copy-start(f32[2,512,384]{2,0,1:T(2,128)} %copy-done.7) | copy-start | bytes 4718596
  301.9 3.6 copy-start.23
  306.6 58.4 %copy-start.17 = (f32[384,1152]{0,1:T(8,128)S(1)}, f32[384,1152]{0,1:T(8,128)}, u32[]{:S(2)}) copy-start(f32[384,1152]{0,1:T(8,128)} %all-gather.5.cloned.1.call-done) | copy-start | bytes 5308420
  312.0 105.2 %all-reduce.25.cloned.1.call-start = ((), (), s32[]{:S(2)}) async-start(), calls=%async_computation.14 | async-start | bytes 1769472 | tf_op jit(solution)/shard_map/psum | solution.py:185
  364.7 99.7 %reduce-scatter.16.cloned.1.call-start = ((), (), s32[]{:S(2)}) async-start(), calls=%async_computation.12 | async-start | bytes 221184
  371.6 45.6 %copy-start.27 = (f32[192,384]{1,0:T(8,128)S(1)}, f32[192,384]{1,0:T(8,128)}, u32[]{:S(2)}) copy-start(f32[192,384]{1,0:T(8,128)} %param.28) | copy-start | bytes 884740
  371.6 47.9 %copy-start.28 = (f32[384,192]{0,1:T(8,128)S(1)}, f32[384,192]{0,1:T(8,128)}, u32[]{:S(2)}) copy-start(f32[384,192]{0,1:T(8,128)} %param.27) | copy-start | bytes 884740
  373.1 49.9 %copy-start.33 = (f32[384,48]{0,1:T(8,128)S(1)}, f32[384,48]{0,1:T(8,128)}, u32[]{:S(2)}) copy-start(f32[384,48]{0,1:T(8,128)} %param.26) | copy-start | bytes 221188
  374.6 143.7 %all-reduce.23.cloned.1.call-start = ((), (), s32[]{:S(2)}) async-start(), calls=%async_computation.13 | async-start | bytes 4718592 | tf_op jit(solution)/shard_map/psum | solution.py:202
  421.2 30.9 %copy-start.30 = (f32[384,192]{0,1:T(8,128)}, f32[384,192]{0,1:T(8,128)S(1)}, u32[]{:S(2)}) copy-start(f32[384,192]{0,1:T(8,128)S(1)} %get-tuple-element.168) | copy-start | bytes 884740
  423.0 190.9 %copy-start.21 = (f32[384,144]{0,1:T(8,128)}, f32[384,144]{0,1:T(8,128)S(1)}, u32[]{:S(2)}) copy-start(f32[384,144]{0,1:T(8,128)S(1)} %get-tuple-element.166) | copy-start | bytes 663556
  424.6 173.7 %copy-start.26 = (f32[384,48]{0,1:T(8,128)}, f32[384,48]{0,1:T(8,128)S(1)}, u32[]{:S(2)}) copy-start(f32[384,48]{0,1:T(8,128)S(1)} %get-tuple-element.167) | copy-start | bytes 221188
  452.1 10.9 %copy-start.6 = (f32[512,384]{0,1:T(8,128)S(1)}, f32[512,384]{0,1:T(8,128)}, u32[]{:S(2)}) copy-start(f32[512,384]{0,1:T(8,128)} %copy-done.5) | copy-start | bytes 2359300
  460.7 14.0 %copy-start.36 = (f32[12,48]{1,0:T(8,128)S(1)}, f32[12,48]{1,0:T(8,128)}, u32[]{:S(2)}) copy-start(f32[12,48]{1,0:T(8,128)} %param.29) | copy-start | bytes 6916
  474.7 51.2 %copy-start.35 = (f32[12,48]{1,0:T(8,128)}, f32[12,48]{1,0:T(8,128)S(1)}, u32[]{:S(2)}) copy-start(f32[12,48]{1,0:T(8,128)S(1)} %psum.95) | copy-start | bytes 6916
  523.4 5.1 copy-start.13
  531.0 5.3 copy-start.12
  538.9 5.1 copy-start.11
  561.2 5.1 copy-start.29
  577.0 5.1 copy-start.31
  609.8 5.5 copy-start.20
  609.8 6.2 copy-start.32
  609.8 6.8 %copy-start.19 = (f32[384,192]{0,1:T(8,128)S(1)}, f32[384,192]{0,1:T(8,128)}, u32[]{:S(2)}) copy-start(f32[384,192]{0,1:T(8,128)} %get-tuple-element.163) | copy-start | bytes 884740
  611.3 6.1 copy-start.18
  (6 other events, 8.5 us)
Sparse Core Ops, SparseCore 0:
  9.7 29.1 all-gather.4
  40.5 35.3 all-gather.6
  77.5 34.0 all-gather.8
  188.1 29.5 reduce-scatter.9
  219.9 34.3 reduce-scatter.11
  256.5 37.8 reduce-scatter.13
  312.1 52.5 reduce-scatter.7
  368.1 49.0 all-reduce.24
  420.1 30.2 reduce-scatter.15
  452.9 65.2 all-reduce.22
